TPU v7x, 32 devices: a whole 2x2x4 slice. The times are simulated.
32 devices in a mesh: pipe: 2 (over x), section: 4 (over y, core), tensor: 4 (over z).
Axes of the slice: x: 2, y: 2, z: 4, core: 2. Of those that a mesh axis runs over, the one named last changes fastest.
Arguments:
- section_input: bfloat16 [2, 4, 384, 2560], P('pipe', 'section', None, 'tensor'), may hold values from -120 to 120
- section_cotan: bfloat16 [2, 4, 384, 2560], P('pipe', 'section', None, 'tensor'), may hold values from -6 to 6
- weights: bfloat16 [6, 2560, 2560], P(None, 'pipe', 'tensor'), may hold values from -0.125 to 0.125
- section_cuts: int32 [3, 5], replicated, may hold values from 0 to 6, as said below
- pipe_template: int32 [2], replicated, may hold values from 0 to 2
Outputs:
- weight_grads: float32 [6, 2560, 2560], P(None, ('pipe', 'section'), 'tensor')
Inputs may be any that keep to these rules, and one draw needn't show every extreme that they name: `section_cuts`: row t starts at 0 and ends with 6; each section holds 1 or 2 layers, and 2 sections of every template hold 2.
All inputs are finite; a program needn't handle non-finite values.
Results may differ from a plain program's by a relative error of at most 0.0039.
Values may be sent and summed in bfloat16 or wider, within the bound.
A program may use at most 128 MiB of HBM per device.

v0:
```python
import jax
import jax.numpy as jnp
from jax import lax
from jax.sharding import PartitionSpec as P

epsilon = 1e-05


def forward_rows(h_cols):
    gathered = lax.all_gather(h_cols, "tensor", axis=1, tiled=True)
    values = gathered.astype(jnp.float32)
    inv_rms = lax.rsqrt(jnp.mean(values * values, axis=1, keepdims=True) + epsilon)
    active = jax.nn.silu(values * inv_rms).astype(jnp.bfloat16)
    return (gathered, inv_rms, active)


def fetch_layer(weights, layer_ids):
    block_rows = jnp.take(weights, layer_ids, axis=0)
    received = lax.all_to_all(block_rows, "pipe", split_axis=0, concat_axis=0, tiled=True)
    return received.reshape(-1, received.shape[2])


def norm_backward(summed, values, inv_rms):
    normed = values * inv_rms
    gate_sig = jax.nn.sigmoid(normed)
    return summed * gate_sig * (1.0 + normed * (1.0 - gate_sig))


def shards(section_input, section_cotan, weights, section_cuts, pipe_template):
    pipe_count = lax.axis_size("pipe")
    sections = lax.axis_size("section")
    layers = weights.shape[0]
    pipe_idx = lax.axis_index("pipe")
    section_idx = lax.axis_index("section")
    template_pick = (
        pipe_template[:, None] == jnp.arange(section_cuts.shape[0], dtype=jnp.int32)[None, :]
    ).astype(jnp.int32)
    starts = jnp.sum(template_pick[:, :, None] * section_cuts[None, :, :sections], axis=1)
    stops = jnp.sum(template_pick[:, :, None] * section_cuts[None, :, 1:], axis=1)
    section_pick = (jnp.arange(sections, dtype=jnp.int32) == section_idx).astype(jnp.int32)
    pipe_pick = (jnp.arange(pipe_count, dtype=jnp.int32) == pipe_idx).astype(jnp.float32)
    here_start = jnp.sum(starts * section_pick[None, :], axis=1)
    here_stop = jnp.sum(stops * section_pick[None, :], axis=1)
    second_ids = jnp.minimum(here_start + 1, layers - 1)
    second_flags = (here_start + 1 < here_stop).astype(jnp.float32)
    my_live = jnp.sum(second_flags * pipe_pick)
    first_matrix = fetch_layer(weights, here_start)
    second_matrix = fetch_layer(weights, second_ids)
    h_first = section_input[0, 0]
    gathered_first, inv_first, active_first = forward_rows(h_first)
    out_first = jnp.dot(active_first, first_matrix, preferred_element_type=jnp.float32)
    h_second = (h_first.astype(jnp.float32) + out_first).astype(jnp.bfloat16)
    gathered_second, inv_second, active_second = forward_rows(h_second)
    cotan_low = section_cotan[0, 0]
    cotan = cotan_low.astype(jnp.float32)
    grad_second = (
        jnp.einsum("td,tc->dc", active_second, cotan_low, preferred_element_type=jnp.float32)
        * my_live
    )
    col_width = h_second.shape[1]
    partial_value = jnp.einsum(
        "tc,dc->td", cotan_low, second_matrix, preferred_element_type=jnp.float32
    )
    summed = lax.psum(partial_value.astype(jnp.bfloat16), "tensor").astype(jnp.float32)
    values = gathered_second.astype(jnp.float32)
    d_norm = norm_backward(summed, values, inv_second)
    mean_term = jnp.mean(values * d_norm, axis=1, keepdims=True)
    d_full = inv_second * d_norm - values * inv_second * inv_second * inv_second * mean_term
    d_rows = lax.dynamic_slice_in_dim(d_full, lax.axis_index("tensor") * col_width, col_width, 1)
    cotan_first = cotan + my_live * d_rows
    grad_first = jnp.einsum(
        "td,tc->dc",
        active_first,
        cotan_first.astype(jnp.bfloat16),
        preferred_element_type=jnp.float32,
    )
    all_first = starts.reshape(-1)
    all_second = jnp.minimum(starts + 1, layers - 1).reshape(-1)
    result = jnp.zeros((layers, weights.shape[1] // sections, weights.shape[2]), jnp.float32)
    for layer_grad, layer_ids in ((grad_first, all_first), (grad_second, all_second)):
        blocks = layer_grad.reshape(pipe_count * sections, -1, layer_grad.shape[1])
        received = lax.all_to_all(
            blocks, ("pipe", "section"), split_axis=0, concat_axis=0, tiled=True
        )
        select = (jnp.arange(layers, dtype=jnp.int32)[:, None] == layer_ids[None, :]).astype(
            jnp.float32
        )
        result = result + jnp.einsum(
            "lq,qrc->lrc", select, received, precision=lax.Precision.HIGHEST
        )
    return result


def solution(mesh):
    in_specs = (
        P("pipe", "section", None, "tensor"),
        P("pipe", "section", None, "tensor"),
        P(None, "pipe", "tensor"),
        P(),
        P(),
    )
    out_specs = P(None, ("pipe", "section"), "tensor")
    return jax.shard_map(shards, mesh=mesh, in_specs=in_specs, out_specs=out_specs, check_vma=False)
```

profile of v0, /device:TPU:0, one launch (start us, length us, event | category | flops | bytes accessed | tf_op | source)
XLA Modules:
  0.0 320.3 jit_solution(11344798411540166552)
XLA Ops:
  6.5 0.7 all-gather.6.cloned.1.call-update
  7.3 0.7 fusion.39
  7.9 0.8 fusion.45
  8.8 0.1 multiply_reduce_fusion.1
  8.8 0.1 multiply_reduce_fusion.3
  9.0 4.9 %gather_fusion = bf16[2,1280,640]{2,1,0:T(8,128)(2,1)S(1)} fusion(bf16[6,1280,640]{2,1,0:T(8,128)(2,1)} %param.9, s32[1024]{0:T(1024)S(1)} %pad_clamp_fusion.1), kind=kCustom, calls=%fused_computation.clone | custom fusion | bytes 6553608 | tf_op jit(solution)/shard_map/jit(_take)/gather | solution.py:18
  14.0 2.1 broadcast_select_fusion.1
  16.1 4.2 %all-to-all-start = ((bf16[2,1280,640]{2,1,0:T(8,128)(2,1)}), bf16[2,1280,640]{2,1,0:T(8,128)(2,1)S(1)}, u32[]{:S(2)}, u32[]{:S(2)}) async-start(bf16[2,1280,640]{2,1,0:T(8,128)(2,1)} %broadcast_select_fusion.1), calls=%async_computation | async-start | bytes 6553600 | tf_op jit(solution)/shard_map/all_to_all | solution.py:19
  20.3 34.8 %all-gather.6.cloned.1.call-done = bf16[1,1,384,2560]{3,2,1,0:T(8,128)(2,1)} async-done(((bf16[1,1,384,640]{3,2,1,0:T(8,128)(2,1)}), bf16[1,1,384,2560]{3,2,1,0:T(8,128)(2,1)}) %all-gather.6.cloned.1.call-update) | async-done | bytes 1966096 | tf_op jit(solution)/shard_map/all_gather | solution.py:10
  55.2 2.0 fusion.10
  57.2 1.9 all-to-all-done
  59.1 4.2 %fusion.18 = bf16[384,640]{1,0:T(8,128)(2,1)} fusion(bf16[2560,640]{1,0:T(8,128)(2,1)S(1)} %bitcast.35, bf16[1,1,384,640]{3,2,1,0:T(8,128)(2,1)} %param.7, bf16[1,1,384,2560]{3,2,1,0:T(8,128)(2,1)} %all-gather.6.cloned.1.call-done, f32[384]{0:T(512)S(1)} %add_rsqrt_fusion.1), kind=kOutput, calls=%fused_computation.31 | convolution fusion | flops 1265909760 | bytes 6227456 | tf_op jit(solution)/shard_map/dot_general | solution.py:51
  63.3 4.9 %gather_fusion.1 = bf16[2,1280,640]{2,1,0:T(8,128)(2,1)S(1)} fusion(bf16[6,1280,640]{2,1,0:T(8,128)(2,1)} %param.9, s32[1024]{0:T(1024)S(1)} %pad_clamp_fusion), kind=kCustom, calls=%fused_computation.1.clone | custom fusion | bytes 6553608 | tf_op jit(solution)/shard_map/jit(_take)/gather | solution.py:18
  68.3 2.1 broadcast_select_fusion
  70.4 4.0 %all-to-all-start.1 = ((bf16[2,1280,640]{2,1,0:T(8,128)(2,1)}), bf16[2,1280,640]{2,1,0:T(8,128)(2,1)S(1)}, u32[]{:S(2)}, u32[]{:S(2)}) async-start(bf16[2,1280,640]{2,1,0:T(8,128)(2,1)} %broadcast_select_fusion), calls=%async_computation.1 | async-start | bytes 6553600 | tf_op jit(solution)/shard_map/all_to_all | solution.py:19
  74.4 0.6 fusion.40
  75.1 32.5 %all-gather.4.cloned.1.call-done = bf16[384,2560]{1,0:T(8,128)(2,1)} async-done(((bf16[384,640]{1,0:T(8,128)(2,1)}), bf16[384,2560]{1,0:T(8,128)(2,1)}) %all-gather.4.cloned.1.call-update) | async-done | bytes 1966096 | tf_op jit(solution)/shard_map/all_gather | solution.py:10
  107.5 2.0 fusion.11
  109.5 7.5 %convolution_multiply_fusion = f32[2560,640]{1,0:T(8,128)} fusion(f32[]{:T(128)} %fusion.40, bf16[1,1,384,640]{3,2,1,0:T(8,128)(2,1)} %param.8, bf16[384,2560]{1,0:T(8,128)(2,1)} %all-gather.4.cloned.1.call-done, f32[384]{0:T(512)S(1)} %add_rsqrt_fusion), kind=kOutput, calls=%fused_computation.9 | convolution fusion | flops 1266810880 | bytes 9012740 | tf_op jit(solution)/shard_map/td,tc->dc/dot_general | solution.py:57
  117.1 1.7 copy-done.1
  118.8 4.8 %all-to-all-start.3 = ((f32[8,320,640]{2,1,0:T(8,128)}), f32[8,320,640]{2,1,0:T(8,128)}, u32[]{:S(2)}, u32[]{:S(2)}) async-start(f32[8,320,640]{2,1,0:T(8,128)} %bitcast.32), calls=%async_computation.3 | async-start | bytes 13107200 | tf_op jit(solution)/shard_map/all_to_all | solution.py:82
  123.6 0.2 all-reduce.2.cloned.1.call-start
  123.8 5.1 %fusion.13 = bf16[384,2560]{1,0:T(8,128)(2,1)} fusion(bf16[2560,640]{1,0:T(8,128)(2,1)} %bitcast.34, bf16[1,1,384,640]{3,2,1,0:T(8,128)(2,1)} %param.8), kind=kOutput, calls=%fused_computation.25 | convolution fusion | flops 1259274240 | bytes 5734400 | tf_op jit(solution)/shard_map/tc,dc->td/dot_general | solution.py:61
  129.0 81.0 %all-reduce.2.cloned.1.call-done = bf16[384,2560]{1,0:T(8,128)(2,1)} async-done(((bf16[384,2560]{1,0:T(8,128)(2,1)}), bf16[384,2560]{1,0:T(8,128)(2,1)}) %all-reduce.2.cloned.1.call-update) | async-done | bytes 1966096 | tf_op jit(solution)/shard_map/psum | solution.py:64
  210.1 3.6 %fusion.12 = (f32[384]{0:T(512)S(1)}, f32[384,2560]{1,0:T(8,128)S(1)}, f32[384,2560]{1,0:T(8,128)S(1)}) fusion(bf16[384,2560]{1,0:T(8,128)(2,1)S(1)} %copy-done, f32[384]{0:T(512)S(1)} %add_rsqrt_fusion, bf16[384,2560]{1,0:T(8,128)(2,1)} %all-reduce.2.cloned.1.call-done), kind=kLoop, calls=%fused_computation.21 | loop fusion | flops 12779136 | bytes 11799552 | tf_op jit(solution)/shard_map/reduce_sum | solution.py:67
  213.7 6.3 %fusion.25 = f32[2560,640]{1,0:T(8,128)} fusion(f32[384,2560]{1,0:T(8,128)S(1)} %get-tuple-element.11, s32[]{:T(128)S(6)} %select_n.10, f32[384,2560]{1,0:T(8,128)S(1)} %get-tuple-element.14, f32[384]{0:T(512)S(1)} %broadcast_multiply_fusion, f32[384]{0:T(512)S(1)} %add_rsqrt_fusion, bf16[1,1,384,640]{3,2,1,0:T(8,128)(2,1)S(1)} %copy-done.3, f32[]{:T(128)} %fusion.40, ...), kind=kOutput, calls=%fused_computation.40 | convolution fusion | flops 1267384320 | bytes 10983432 | tf_op jit(solution)/shard_map/td,tc->dc/dot_general | solution.py:71
  220.0 5.0 %all-to-all-start.2 = ((f32[8,320,640]{2,1,0:T(8,128)}), f32[8,320,640]{2,1,0:T(8,128)}, u32[]{:S(2)}, u32[]{:S(2)}) async-start(f32[8,320,640]{2,1,0:T(8,128)} %bitcast.33), calls=%async_computation.2 | async-start | bytes 13107200 | tf_op jit(solution)/shard_map/all_to_all | solution.py:82
  225.0 0.1 eq.65
  225.1 12.2 %fusion = f32[6,320,640]{2,0,1:T(8,128)} fusion(f32[8,320,640]{2,1,0:T(8,128)} %all-to-all-done.3, s32[8]{0:T(128)S(1)} %add_minimum_fusion), kind=kOutput, calls=%fused_computation.2 | convolution fusion | flops 117964848 | bytes 11468832 | tf_op jit(solution)/shard_map/lq,qrc->lrc/dot_general | solution.py:88
  237.3 61.0 %all-to-all-done.2 = f32[8,320,640]{2,1,0:T(8,128)} async-done(((f32[8,320,640]{2,1,0:T(8,128)}), f32[8,320,640]{2,1,0:T(8,128)}, u32[]{:S(2)}, u32[]{:S(2)}) %all-to-all-start.2) | async-done | bytes 6553632 | tf_op jit(solution)/shard_map/all_to_all | solution.py:82
  298.3 12.3 %fusion.14 = f32[6,320,640]{2,0,1:T(8,128)S(1)} fusion(f32[6,320,640]{2,0,1:T(8,128)} %fusion, f32[8,320,640]{2,1,0:T(8,128)} %all-to-all-done.2, s32[8]{0:T(128)S(1)} %eq.65), kind=kOutput, calls=%fused_computation.28 | convolution fusion | flops 119193648 | bytes 16384032 | tf_op jit(solution)/shard_map/lq,qrc->lrc/dot_general | solution.py:88
  310.6 3.1 copy.17
  (22 shorter events, 0.1 us)
Async XLA Ops:
  6.5 48.6 %all-gather.6.cloned.1.call-start = ((), (), s32[]{:S(2)}) async-start(), calls=%async_computation.6 | async-start | bytes 2457600 | tf_op jit(solution)/shard_map/all_gather | solution.py:10
  16.1 43.0 %all-to-all-start = ((bf16[2,1280,640]{2,1,0:T(8,128)(2,1)}), bf16[2,1280,640]{2,1,0:T(8,128)(2,1)S(1)}, u32[]{:S(2)}, u32[]{:S(2)}) async-start(bf16[2,1280,640]{2,1,0:T(8,128)(2,1)} %broadcast_select_fusion.1), calls=%async_computation | async-start | bytes 6553600 | tf_op jit(solution)/shard_map/all_to_all | solution.py:19
  20.3 87.2 %all-gather.4.cloned.1.call-start = ((), (), s32[]{:S(2)}) async-start(), calls=%async_computation.4 | async-start | bytes 2457600 | tf_op jit(solution)/shard_map/all_gather | solution.py:10
  70.4 46.7 %all-to-all-start.1 = ((bf16[2,1280,640]{2,1,0:T(8,128)(2,1)}), bf16[2,1280,640]{2,1,0:T(8,128)(2,1)S(1)}, u32[]{:S(2)}, u32[]{:S(2)}) async-start(bf16[2,1280,640]{2,1,0:T(8,128)(2,1)} %broadcast_select_fusion), calls=%async_computation.1 | async-start | bytes 6553600 | tf_op jit(solution)/shard_map/all_to_all | solution.py:19
  117.1 1.7 copy-start.1
  118.8 101.2 %all-to-all-start.3 = ((f32[8,320,640]{2,1,0:T(8,128)}), f32[8,320,640]{2,1,0:T(8,128)}, u32[]{:S(2)}, u32[]{:S(2)}) async-start(f32[8,320,640]{2,1,0:T(8,128)} %bitcast.32), calls=%async_computation.3 | async-start | bytes 13107200 | tf_op jit(solution)/shard_map/all_to_all | solution.py:82
  123.6 86.5 %all-reduce.2.cloned.1.call-start = ((), (), s32[]{:S(2)}) async-start(), calls=%async_computation.5 | async-start | bytes 3932160 | tf_op jit(solution)/shard_map/psum | solution.py:64
  123.8 86.2 %copy-start = (bf16[384,2560]{1,0:T(8,128)(2,1)S(1)}, bf16[384,2560]{1,0:T(8,128)(2,1)}, u32[]{:S(2)}) copy-start(bf16[384,2560]{1,0:T(8,128)(2,1)} %all-gather.4.cloned.1.call-done) | copy-start | bytes 5898244
  129.0 84.7 %copy-start.3 = (bf16[1,1,384,640]{3,2,1,0:T(8,128)(2,1)S(1)}, bf16[1,1,384,640]{3,2,1,0:T(8,128)(2,1)}, u32[]{:S(2)}) copy-start(bf16[1,1,384,640]{3,2,1,0:T(8,128)(2,1)} %param.8) | copy-start | bytes 1474564
  210.0 3.7 %copy-start.2 = (bf16[1,1,384,2560]{3,2,1,0:T(8,128)(2,1)S(1)}, bf16[1,1,384,2560]{3,2,1,0:T(8,128)(2,1)}, u32[]{:S(2)}) copy-start(bf16[1,1,384,2560]{3,2,1,0:T(8,128)(2,1)} %all-gather.6.cloned.1.call-done) | copy-start | bytes 5898244
  220.0 78.3 %all-to-all-start.2 = ((f32[8,320,640]{2,1,0:T(8,128)}), f32[8,320,640]{2,1,0:T(8,128)}, u32[]{:S(2)}, u32[]{:S(2)}) async-start(f32[8,320,640]{2,1,0:T(8,128)} %bitcast.33), calls=%async_computation.2 | async-start | bytes 13107200 | tf_op jit(solution)/shard_map/all_to_all | solution.py:82
Sparse Core Ops, SparseCore 0:
  8.9 46.2 all-gather.5
  63.4 44.0 all-gather.3
  129.1 80.8 all-reduce.1
where the time goes:
time: 321 us; the launch traced here: 320 us
  waiting for transfers between devices  212 us (66%)
  matrix products  47.6 us (15%)
  starting transfers between devices  18.3 us (6%)
  local copies, waits for them, and re-layouts  15.7 us (5%)
  other arithmetic  13.5 us (4%)
  between operations  13.2 us (4%)
    psum x1, waiting for transfers between devices, shards(): lax.psum(partial_value.astype(jnp.bfloat16), 'tensor').astype(jnp.float32)  81 us
    all_gather x2, waiting for transfers between devices, forward_rows(): gathered = lax.all_gather(h_cols, 'tensor', axis=1, tiled=True)  67.3 us
    all_to_all x2, waiting for transfers between devices, shards(): lax.all_to_all(blocks, ('pipe', 'section'), split_axis=0, concat_axis=0,...  61 us
    dot_general x2, matrix products, shards(): jnp.einsum('lq,qrc->lrc', select, received, precision=lax.Precision.HIGHEST)  24.5 us
    gather x2, local copies, waits for them, and re-layouts, fetch_layer(): block_rows = jnp.take(weights, layer_ids, axis=0)  9.9 us
    all_to_all x2, starting transfers between devices, shards(): lax.all_to_all(blocks, ('pipe', 'section'), split_axis=0, concat_axis=0,...  9.78 us
    all_to_all x2, starting transfers between devices, fetch_layer(): lax.all_to_all(block_rows, 'pipe', split_axis=0, concat_axis=0, tiled=True)  8.25 us
    dot_general x1, matrix products, shards(): jnp.einsum('td,tc->dc', active_second, cotan_low, preferred_element_type=...  7.55 us
  transfers between devices with their start and end apart: 7, of which 5 were waited for; matrix products, arithmetic and copies ran while one was open for 17% of the time, Pallas kernels for 0%

commit v1 on v0

--- a/solution.py
+++ b/solution.py
@@ -14,10 +14,40 @@
     return (gathered, inv_rms, active)
 
 
-def fetch_layer(weights, layer_ids):
-    block_rows = jnp.take(weights, layer_ids, axis=0)
+def fetch_layer(weights, layer_ids, pipe_count, pipe_idx):
+    if pipe_count == 2:
+        own = lax.dynamic_index_in_dim(weights, layer_ids[pipe_idx], 0, keepdims=False)
+        peer = lax.dynamic_index_in_dim(weights, layer_ids[1 - pipe_idx], 0, keepdims=False)
+        other = lax.ppermute(peer, "pipe", [(0, 1), (1, 0)])
+        return own, other
+    block_rows = jnp.take(weights, layer_ids, axis=0, mode="clip")
     received = lax.all_to_all(block_rows, "pipe", split_axis=0, concat_axis=0, tiled=True)
-    return received.reshape(-1, received.shape[2])
+    return (received.reshape(-1, received.shape[2]),)
+
+
+def forward_product(active, parts, pipe_idx):
+    if len(parts) == 1:
+        return jnp.dot(active, parts[0], preferred_element_type=jnp.float32)
+    rows = parts[0].shape[0]
+    mine = lax.dynamic_slice_in_dim(active, pipe_idx * rows, rows, 1)
+    rest = lax.dynamic_slice_in_dim(active, (1 - pipe_idx) * rows, rows, 1)
+    return jnp.dot(mine, parts[0], preferred_element_type=jnp.float32) + jnp.dot(
+        rest, parts[1], preferred_element_type=jnp.float32
+    )
+
+
+def backward_product(cotan, parts, pipe_idx):
+    out = [
+        jnp.einsum("tc,dc->td", cotan, part, preferred_element_type=jnp.float32).astype(
+            jnp.bfloat16
+        )
+        for part in parts
+    ]
+    if len(out) == 1:
+        return out[0]
+    low = jnp.where(pipe_idx == 0, out[0], out[1])
+    high = jnp.where(pipe_idx == 0, out[1], out[0])
+    return jnp.concatenate([low, high], axis=1)
 
 
 def norm_backward(summed, values, inv_rms):
@@ -44,11 +74,11 @@
     second_ids = jnp.minimum(here_start + 1, layers - 1)
     second_flags = (here_start + 1 < here_stop).astype(jnp.float32)
     my_live = jnp.sum(second_flags * pipe_pick)
-    first_matrix = fetch_layer(weights, here_start)
-    second_matrix = fetch_layer(weights, second_ids)
+    first_parts = fetch_layer(weights, here_start, pipe_count, pipe_idx)
+    second_parts = fetch_layer(weights, second_ids, pipe_count, pipe_idx)
     h_first = section_input[0, 0]
     gathered_first, inv_first, active_first = forward_rows(h_first)
-    out_first = jnp.dot(active_first, first_matrix, preferred_element_type=jnp.float32)
+    out_first = forward_product(active_first, first_parts, pipe_idx)
     h_second = (h_first.astype(jnp.float32) + out_first).astype(jnp.bfloat16)
     gathered_second, inv_second, active_second = forward_rows(h_second)
     cotan_low = section_cotan[0, 0]
@@ -58,15 +88,16 @@
         * my_live
     )
     col_width = h_second.shape[1]
-    partial_value = jnp.einsum(
-        "tc,dc->td", cotan_low, second_matrix, preferred_element_type=jnp.float32
+    partial_value = backward_product(cotan_low, second_parts, pipe_idx)
+    summed = lax.psum_scatter(
+        partial_value, "tensor", scatter_dimension=1, tiled=True
+    ).astype(jnp.float32)
+    values = h_second.astype(jnp.float32)
+    d_norm = norm_backward(summed, values, inv_second)
+    mean_term = lax.psum(jnp.sum(values * d_norm, axis=1), "tensor")[:, None] / (
+        col_width * lax.axis_size("tensor")
     )
-    summed = lax.psum(partial_value.astype(jnp.bfloat16), "tensor").astype(jnp.float32)
-    values = gathered_second.astype(jnp.float32)
-    d_norm = norm_backward(summed, values, inv_second)
-    mean_term = jnp.mean(values * d_norm, axis=1, keepdims=True)
-    d_full = inv_second * d_norm - values * inv_second * inv_second * inv_second * mean_term
-    d_rows = lax.dynamic_slice_in_dim(d_full, lax.axis_index("tensor") * col_width, col_width, 1)
+    d_rows = inv_second * d_norm - values * inv_second * inv_second * inv_second * mean_term
     cotan_first = cotan + my_live * d_rows
     grad_first = jnp.einsum(
         "td,tc->dc",
@@ -76,19 +107,26 @@
     )
     all_first = starts.reshape(-1)
     all_second = jnp.minimum(starts + 1, layers - 1).reshape(-1)
-    result = jnp.zeros((layers, weights.shape[1] // sections, weights.shape[2]), jnp.float32)
-    for layer_grad, layer_ids in ((grad_first, all_first), (grad_second, all_second)):
-        blocks = layer_grad.reshape(pipe_count * sections, -1, layer_grad.shape[1])
-        received = lax.all_to_all(
-            blocks, ("pipe", "section"), split_axis=0, concat_axis=0, tiled=True
+    pieces = []
+    for layer_grad in (grad_first, grad_second):
+        blocks = layer_grad.astype(jnp.bfloat16).reshape(
+            pipe_count * sections, -1, layer_grad.shape[1]
         )
-        select = (jnp.arange(layers, dtype=jnp.int32)[:, None] == layer_ids[None, :]).astype(
-            jnp.float32
+        pieces.append(
+            lax.all_to_all(
+                blocks, ("pipe", "section"), split_axis=0, concat_axis=0, tiled=True
+            )
         )
-        result = result + jnp.einsum(
-            "lq,qrc->lrc", select, received, precision=lax.Precision.HIGHEST
-        )
-    return result
+    select = (
+        jnp.arange(layers, dtype=jnp.int32)[:, None]
+        == jnp.concatenate([all_first, all_second])[None, :]
+    ).astype(jnp.bfloat16)
+    count = all_first.shape[0]
+    return jnp.einsum(
+        "lq,qrc->lrc", select[:, :count], pieces[0], preferred_element_type=jnp.float32
+    ) + jnp.einsum(
+        "lq,qrc->lrc", select[:, count:], pieces[1], preferred_element_type=jnp.float32
+    )
 
 
 def solution(mesh):

time: 321 us -> 231 us (0.72)
  waiting for transfers between devices: 212 us -> 132 us
  matrix products: 47.6 us -> 34.3 us
  blocking collectives: 0 us -> 10.2 us
  between operations: 13.2 us -> 20.9 us
  local copies, waits for them, and re-layouts: 15.7 us -> 9 us
  starting transfers between devices: 18.3 us -> 12.8 us
    psum x1 -> x0, waiting for transfers between devices: 81 us -> none  [shards(): lax.psum(partial_value.astype(jnp.bfloat16), 'tensor').astype(jnp.float32)]
    ppermute x0 -> x2, waiting for transfers between devices: none -> 30.7 us  [fetch_layer(): other = lax.ppermute(peer, 'pipe', [(0, 1), (1, 0)])]
    unnamed x3 -> x4, waiting for transfers between devices: 0.74 us -> 31.4 us
    all_gather x2, waiting for transfers between devices: 67.3 us -> 36.8 us  [forward_rows(): gathered = lax.all_gather(h_cols, 'tensor', axis=1, tiled=True)]
    all_to_all x2, waiting for transfers between devices: 61 us -> 33.4 us  [shards(): lax.all_to_all(blocks, ('pipe', 'section'), split_axis=0, concat_axis=0,...]
    dot_general x4 -> x6, matrix products: 33.8 us -> 21.1 us  [the longest x1 6.14 us: shards(): jnp.einsum('lq,qrc->lrc', select[:, :count], pieces[0], preferred_element...]
    psum x0 -> x1, blocking collectives: none -> 10.2 us  [shards(): lax.psum(jnp.sum(values * d_norm, axis=1), 'tensor')[:, None]]
    gather x2 -> x0, local copies, waits for them, and re-layouts: 9.9 us -> none  [fetch_layer(): block_rows = jnp.take(weights, layer_ids, axis=0)]
  transfers between devices with their start and end apart: 7 -> 7, of which waited for: 5 -> 5; matrix products, arithmetic and copies ran while one was open for 17% -> 18% of each run, Pallas kernels for 0% -> 0%
where the time goes in v1:
time: 231 us; the launch traced here: 230 us
  waiting for transfers between devices  132 us (57%)
  matrix products  34.3 us (15%)
  between operations  20.9 us (9%)
  starting transfers between devices  12.8 us (6%)
  other arithmetic  10.7 us (5%)
  blocking collectives  10.2 us (4%)
  local copies, waits for them, and re-layouts  9 us (4%)
    all_gather x2, waiting for transfers between devices, forward_rows(): gathered = lax.all_gather(h_cols, 'tensor', axis=1, tiled=True)  36.8 us
    all_to_all x2, waiting for transfers between devices, shards(): lax.all_to_all(blocks, ('pipe', 'section'), split_axis=0, concat_axis=0,...  33.4 us
    unnamed x4, waiting for transfers between devices  31.4 us
    ppermute x2, waiting for transfers between devices, fetch_layer(): other = lax.ppermute(peer, 'pipe', [(0, 1), (1, 0)])  30.7 us
    psum x1, blocking collectives, shards(): lax.psum(jnp.sum(values * d_norm, axis=1), 'tensor')[:, None]  10.2 us
    all_to_all x2, starting transfers between devices, shards(): lax.all_to_all(blocks, ('pipe', 'section'), split_axis=0, concat_axis=0,...  8.13 us
    dot_general x1, matrix products, shards(): jnp.einsum('td,tc->dc', active_first, cotan_first.astype(jnp.bfloat16), p...  6.76 us
    dot_general x1, matrix products, shards(): jnp.einsum('td,tc->dc', active_second, cotan_low, preferred_element_type=...  6.45 us
  transfers between devices with their start and end apart: 7, of which 5 were waited for; matrix products, arithmetic and copies ran while one was open for 18% of the time, Pallas kernels for 0%

profile of v1, /device:TPU:0, one launch (start us, length us, event | category | flops | bytes accessed | tf_op | source)
XLA Modules:
  0.0 230.1 jit_solution(14350900138296770792)
XLA Ops:
  6.5 0.7 all-gather.6.cloned.1.call-update
  7.3 0.7 fusion.61
  8.0 0.8 fusion.68
  8.9 0.1 multiply_reduce_fusion.3
  9.1 0.7 fusion.69
  13.5 2.2 dynamic-slice_bitcast_fusion
  15.7 3.0 %collective-permute-start = (bf16[1280,640]{1,0:T(8,128)(2,1)S(1)}, bf16[1280,640]{1,0:T(8,128)(2,1)}, u32[]{:S(2)}, u32[]{:S(2)}) collective-permute-start(bf16[1280,640]{1,0:T(8,128)(2,1)S(1)} %get-tuple-element.10), channel_id=1, source_target_pairs={{0,16},{16,0},{1,17},{17,1},{2,18},{18,2},{3,19},{19,3},{4,20},{20... | collective-permute-start | bytes 4915208 | tf_op jit(solution)/shard_map/ppermute | solution.py:21
  20.6 34.5 %all-gather.6.cloned.1.call-done = bf16[1,1,384,2560]{3,2,1,0:T(8,128)(2,1)} async-done(((bf16[1,1,384,640]{3,2,1,0:T(8,128)(2,1)}), bf16[1,1,384,2560]{3,2,1,0:T(8,128)(2,1)}) %all-gather.6.cloned.1.call-update) | async-done | bytes 1966096 | tf_op jit(solution)/shard_map/all_gather | solution.py:10
  55.2 2.1 fusion.13
  57.3 1.5 fusion.7
  58.9 3.1 %fusion.25 = f32[384,640]{1,0:T(8,128)S(1)} fusion(bf16[6,1280,640]{2,1,0:T(8,128)(2,1)} %param.7, s32[]{:T(128)S(6)} %select_n.47, bf16[384,2560]{1,0:T(8,128)(2,1)S(1)} %fusion.7, s32[]{:T(128)S(6)} %select_n.45), kind=kOutput, calls=%fused_computation.31 | convolution fusion | flops 629145600 | bytes 3604488 | tf_op jit(solution)/shard_map/dot_general | solution.py:34
  62.0 3.2 %fusion.30 = bf16[384,640]{1,0:T(8,128)(2,1)} fusion(f32[384,640]{1,0:T(8,128)S(1)} %fusion.25, bf16[1280,640]{1,0:T(8,128)(2,1)} %collective-permute-done, bf16[384,2560]{1,0:T(8,128)(2,1)S(1)} %fusion.7, s32[]{:T(128)S(6)} %select_n.48, bf16[1,1,384,640]{3,2,1,0:T(8,128)(2,1)S(1)} %copy-done.2), kind=kOutput, calls=%fused_computation.39 | convolution fusion | flops 630128640 | bytes 4587524 | tf_op jit(solution)/shard_map/dot_general | solution.py:34
  65.2 1.5 collective-permute-start.1
  68.7 2.7 %convolution_convert_fusion.2 = bf16[1280,384]{1,0:T(8,128)(2,1)S(1)} fusion(bf16[6,1280,640]{2,1,0:T(8,128)(2,1)} %param.7, s32[]{:T(128)S(6)} %select_n.52, bf16[1,1,384,640]{3,2,1,0:T(8,128)(2,1)} %param.6), kind=kOutput, calls=%fused_computation.25 | convolution fusion | flops 629637120 | bytes 3112964 | tf_op jit(solution)/shard_map/tc,dc->td/dot_general | solution.py:41
  71.4 30.7 %collective-permute-done.1 = bf16[1280,640]{1,0:T(8,128)(2,1)S(1)} collective-permute-done((bf16[1280,640]{1,0:T(8,128)(2,1)S(1)}, bf16[1280,640]{1,0:T(8,128)(2,1)S(1)}, u32[]{:S(2)}, u32[]{:S(2)}) %collective-permute-start.1) | collective-permute-done | bytes 1638432 | tf_op jit(solution)/shard_map/ppermute | solution.py:21
  102.1 1.2 select_bitcast_fusion.1
  103.3 1.5 maximum_bitcast_fusion
  104.8 0.6 fusion.65
  105.4 2.2 all-gather.4.cloned.1.call-done
  107.7 2.0 fusion.12
  109.7 6.4 %multiply_convert_fusion = bf16[2560,640]{1,0:T(8,128)(2,1)} fusion(f32[]{:T(128)} %fusion.65, bf16[384,2560]{1,0:T(8,128)(2,1)} %all-gather.4.cloned.1.call-done, f32[384]{0:T(512)S(1)} %add_rsqrt_fusion, bf16[1,1,384,640]{3,2,1,0:T(8,128)(2,1)S(1)} %copy-done.4), kind=kOutput, calls=%fused_computation | convolution fusion | flops 1268449280 | bytes 5735940 | tf_op jit(solution)/shard_map/td,tc->dc/dot_general | solution.py:87
  116.1 3.7 %all-to-all-start.1 = ((bf16[8,320,640]{2,1,0:T(8,128)(2,1)}), bf16[8,320,640]{2,1,0:T(8,128)(2,1)S(1)}, u32[]{:S(2)}, u32[]{:S(2)}) async-start(bf16[8,320,640]{2,1,0:T(8,128)(2,1)} %bitcast.53), calls=%async_computation.1 | async-start | bytes 6553600 | tf_op jit(solution)/shard_map/all_to_all | solution.py:116
  119.8 30.6 %reduce-scatter.4.cloned.1.call-done = bf16[640,384]{1,0:T(8,128)(2,1)} async-done(((bf16[2560,384]{1,0:T(8,128)(2,1)}), bf16[640,384]{1,0:T(8,128)(2,1)}) %reduce-scatter.4.cloned.1.call-update) | async-done | bytes 491536
  150.4 2.0 copy.20
  152.5 1.9 fusion.45
  154.4 10.2 %psum.7 = f32[384]{0:T(512)S(1)} all-reduce(f32[384]{0:T(512)S(1)} %fusion.45), channel_id=1, replica_groups=mesh['pipe'=2,'section'=4,'tensor'=4] {'tensor'}, use_global_device_ids=true, to_apply=%region_9.10 | all-reduce | flops 384 | bytes 3072 | tf_op jit(solution)/shard_map/psum | solution.py:97
  164.7 6.8 %convolution_convert_fusion = bf16[2560,640]{1,0:T(8,128)(2,1)} fusion(bf16[384,2560]{1,0:T(8,128)(2,1)} %copy-done.1, bf16[384,640]{1,0:T(8,128)(2,1)} %fusion.30, bf16[1,1,384,640]{3,2,1,0:T(8,128)(2,1)} %param.6, f32[384]{0:T(512)S(1)} %broadcast_multiply_fusion, f32[384]{0:T(512)S(1)} %add_rsqrt_fusion, f32[]{:T(128)} %fusion.65, bf16[384,640]{1,0:T(8,128)(2,1)} %copy.20), kind=kOutput, calls=%fused_computation.5 | convolution fusion | flops 1264844800 | bytes 6720516 | tf_op jit(solution)/shard_map/td,tc->dc/dot_general | solution.py:102
  171.4 4.5 %all-to-all-start = ((bf16[8,320,640]{2,1,0:T(8,128)(2,1)}), bf16[8,320,640]{2,1,0:T(8,128)(2,1)}, u32[]{:S(2)}, u32[]{:S(2)}) async-start(bf16[8,320,640]{2,1,0:T(8,128)(2,1)} %bitcast.52), calls=%async_computation | async-start | bytes 6553600 | tf_op jit(solution)/shard_map/all_to_all | solution.py:116
  176.1 4.8 %fusion.14 = f32[6,320,640]{2,0,1:T(8,128)} fusion(bf16[8,320,640]{2,1,0:T(8,128)(2,1)S(1)} %all-to-all-done.1, pred[6,16]{1,0:T(8,128)(4,1)S(1)} %iota_compare_fusion), kind=kOutput, calls=%fused_computation.20 | convolution fusion | flops 19660800 | bytes 8192096 | tf_op jit(solution)/shard_map/lq,qrc->lrc/dot_general | solution.py:127
  180.8 33.4 %all-to-all-done = bf16[8,320,640]{2,1,0:T(8,128)(2,1)} async-done(((bf16[8,320,640]{2,1,0:T(8,128)(2,1)}), bf16[8,320,640]{2,1,0:T(8,128)(2,1)}, u32[]{:S(2)}, u32[]{:S(2)}) %all-to-all-start) | async-done | bytes 3276832 | tf_op jit(solution)/shard_map/all_to_all | solution.py:116
  214.3 6.1 %fusion.18 = f32[6,320,640]{2,0,1:T(8,128)S(1)} fusion(f32[6,320,640]{2,0,1:T(8,128)} %fusion.14, bf16[8,320,640]{2,1,0:T(8,128)(2,1)} %all-to-all-done, pred[6,16]{1,0:T(8,128)(4,1)S(1)} %iota_compare_fusion), kind=kOutput, calls=%fused_computation.26 | convolution fusion | flops 20889600 | bytes 13107296 | tf_op jit(solution)/shard_map/lq,qrc->lrc/dot_general | solution.py:125
  220.4 3.1 %copy.18 = f32[6,320,640]{2,1,0:T(8,128)} copy(f32[6,320,640]{2,0,1:T(8,128)S(1)} %fusion.18) | data formatting | bytes 9830400 | tf_op jit(solution)/shard_map/add | solution.py:125
  (27 shorter events, 0.4 us)
Async XLA Ops:
  6.5 48.6 %all-gather.6.cloned.1.call-start = ((), (), s32[]{:S(2)}) async-start(), calls=%async_computation.4 | async-start | bytes 2457600 | tf_op jit(solution)/shard_map/all_gather | solution.py:10
  7.3 100.4 %all-gather.4.cloned.1.call-start = ((), (), s32[]{:S(2)}) async-start(), calls=%async_computation.3 | async-start | bytes 2457600 | tf_op jit(solution)/shard_map/all_gather | solution.py:10
  15.7 46.2 %collective-permute-start = (bf16[1280,640]{1,0:T(8,128)(2,1)S(1)}, bf16[1280,640]{1,0:T(8,128)(2,1)}, u32[]{:S(2)}, u32[]{:S(2)}) collective-permute-start(bf16[1280,640]{1,0:T(8,128)(2,1)S(1)} %get-tuple-element.10), channel_id=1, source_target_pairs={{0,16},{16,0},{1,17},{17,1},{2,18},{18,2},{3,19},{19,3},{4,20},{20... | collective-permute-start | bytes 4915208 | tf_op jit(solution)/shard_map/ppermute | solution.py:21
  55.2 2.2 copy-start
  57.3 4.6 %copy-start.2 = (bf16[1,1,384,640]{3,2,1,0:T(8,128)(2,1)S(1)}, bf16[1,1,384,640]{3,2,1,0:T(8,128)(2,1)}, u32[]{:S(2)}) copy-start(bf16[1,1,384,640]{3,2,1,0:T(8,128)(2,1)} %param.5) | copy-start | bytes 1474564
  58.8 3.1 %copy-start.1 = (bf16[384,2560]{1,0:T(8,128)(2,1)}, bf16[384,2560]{1,0:T(8,128)(2,1)S(1)}, u32[]{:S(2)}) copy-start(bf16[384,2560]{1,0:T(8,128)(2,1)S(1)} %fusion.7) | copy-start | bytes 5898244
  65.2 85.3 %reduce-scatter.4.cloned.1.call-start = ((), (), s32[]{:S(2)}) async-start(), calls=%async_computation.5 | async-start | bytes 2457600
  65.2 36.8 %collective-permute-start.1 = (bf16[1280,640]{1,0:T(8,128)(2,1)S(1)}, bf16[1280,640]{1,0:T(8,128)(2,1)S(1)}, u32[]{:S(2)}, u32[]{:S(2)}) collective-permute-start(bf16[1280,640]{1,0:T(8,128)(2,1)S(1)} %get-tuple-element.9), channel_id=1, source_target_pairs={{0,16},{16,0},{1,17},{17,1},{2,18},{18,2},{3,19},{19,3},{4,20},{20... | collective-permute-start | bytes 4915208 | tf_op jit(solution)/shard_map/ppermute | solution.py:21
  68.7 33.4 %copy-start.3 = (bf16[1,1,384,640]{3,2,1,0:T(8,128)(2,1)S(1)}, bf16[1,1,384,640]{3,2,1,0:T(8,128)(2,1)}, u32[]{:S(2)}) copy-start(bf16[1,1,384,640]{3,2,1,0:T(8,128)(2,1)} %param.6) | copy-start | bytes 1474564
  103.3 6.4 %copy-start.4 = (bf16[1,1,384,640]{3,2,1,0:T(8,128)(2,1)S(1)}, bf16[1,1,384,640]{3,2,1,0:T(8,128)(2,1)}, u32[]{:S(2)}) copy-start(bf16[1,1,384,640]{3,2,1,0:T(8,128)(2,1)} %param.6) | copy-start | bytes 1474564
  116.1 55.3 %all-to-all-start.1 = ((bf16[8,320,640]{2,1,0:T(8,128)(2,1)}), bf16[8,320,640]{2,1,0:T(8,128)(2,1)S(1)}, u32[]{:S(2)}, u32[]{:S(2)}) async-start(bf16[8,320,640]{2,1,0:T(8,128)(2,1)} %bitcast.53), calls=%async_computation.1 | async-start | bytes 6553600 | tf_op jit(solution)/shard_map/all_to_all | solution.py:116
  171.4 42.8 %all-to-all-start = ((bf16[8,320,640]{2,1,0:T(8,128)(2,1)}), bf16[8,320,640]{2,1,0:T(8,128)(2,1)}, u32[]{:S(2)}, u32[]{:S(2)}) async-start(bf16[8,320,640]{2,1,0:T(8,128)(2,1)} %bitcast.52), calls=%async_computation | async-start | bytes 6553600 | tf_op jit(solution)/shard_map/all_to_all | solution.py:116
Sparse Core Ops, SparseCore 0:
  8.9 46.2 all-gather.5
  65.3 42.3 all-gather.3
  110.0 40.4 reduce-scatter.3
